TPU v7x, 32 devices: a whole 2x2x4 slice. The times are simulated.
32 devices in a mesh: band: 4 (over z), roster: 8 (over y, x, core).
Axes of the slice: x: 2, y: 2, z: 4, core: 2. Of those that a mesh axis runs over, the one named last changes fastest.
Arguments:
- tiles: bfloat16 [4, 8, 6, 256, 256], P('band', 'roster'), as said below
- tile_slots: int32 [4, 8, 6], P('band', 'roster'), may hold values from 0 to 5, each once within a row
- tile_count: int32 [4, 8], P('band', 'roster'), may hold values from 1 to 6, as said below
- costs: float32 [6144, 128], P('roster'), may hold values from 1000 to 10000
- primal_start: float32 [6144, 128], P('roster'), may hold values from 0 to 1
- dual_start: float32 [2048, 128], P('band'), may hold values from 0.5 to 4
Outputs:
- primal: float32 [6144, 128], P('roster')
- dual: float32 [2048, 128], P('band')
Inputs may be any that keep to these rules, and one draw needn't show every extreme that they name: `tile_slots`: each device's slots list every tile position once; slot s is in use where s < tile_count. `tile_count`: some device uses all 6 slots. `tiles`: entries are zero or positive.
All inputs are finite; a program needn't handle non-finite values.
Results may differ from a plain program's by a relative error of at most 0.0003.
Values sent between devices are 32-bit elements; how exact they have to be, the bound alone decides.
A program may use at most 64 MiB of HBM per device.

v0:
```python
import jax
import jax.numpy as jnp
from jax import lax
from jax.sharding import PartitionSpec as P

ROUNDS = 3
ITERS = 4
HIGH = lax.Precision.HIGHEST
eps = 1e-06


def shards(tiles, tile_slots, tile_count, costs, primal_start, dual_start):
    tile_block = tiles[0, 0]
    slots = tile_slots[0, 0]
    count = tile_count[0, 0]
    tile = tile_block.shape[1]
    rows = dual_start.shape[0]
    cols = costs.shape[0]
    row_tiles = rows // tile
    col_tiles = cols // tile
    row_index = slots // col_tiles
    col_index = slots % col_tiles
    active = (jnp.arange(slots.shape[0], dtype=jnp.int32) < count).astype(jnp.float32)
    row_hot = (row_index[None, :] == jnp.arange(row_tiles, dtype=jnp.int32)[:, None]).astype(
        jnp.float32
    )
    col_hot = (col_index[None, :] == jnp.arange(col_tiles, dtype=jnp.int32)[:, None]).astype(
        jnp.float32
    )

    def scale_tiles(row_scale, col_scale):
        row_part = row_scale.reshape(row_tiles, tile)[row_index]
        col_part = col_scale.reshape(col_tiles, tile)[col_index]
        return (
            tile_block.astype(jnp.float32)
            * row_part[:, :, None]
            * col_part[:, None, :]
            * active[:, None, None]
        )

    row_scale = jnp.ones((rows,), jnp.float32)
    col_scale = jnp.ones((cols,), jnp.float32)
    for turn in range(ROUNDS):
        magnitude = jnp.abs(scale_tiles(row_scale, col_scale))
        slot_rows = jnp.max(magnitude, axis=2)
        slot_cols = jnp.max(magnitude, axis=1)
        row_peak = jnp.max(row_hot[:, :, None] * slot_rows[None], axis=1).reshape(-1)
        col_peak = jnp.max(col_hot[:, :, None] * slot_cols[None], axis=1).reshape(-1)
        row_peak = lax.pmax(row_peak, "roster")
        col_peak = lax.pmax(col_peak, "band")
        row_scale = row_scale / jnp.sqrt(row_peak + eps)
        col_scale = col_scale / jnp.sqrt(col_peak + eps)
    scaled = scale_tiles(row_scale, col_scale)
    squares = lax.psum(jnp.sum(scaled * scaled), ("band", "roster"))
    eta = 0.9 / jnp.sqrt(squares + eps)
    scen = costs.shape[1]
    col_full = col_scale[:, None]
    row_full = row_scale[:, None]
    cost_t = costs * col_full
    upper = 1.0 / col_full
    primal = primal_start / col_full
    dual = dual_start / row_full
    for step in range(ITERS):
        dual_slots = dual.reshape(row_tiles, tile, scen)[row_index]
        back_terms = jnp.einsum("sij,sik->sjk", scaled, dual_slots, precision=HIGH)
        g_local = jnp.einsum("cs,sjk->cjk", col_hot, back_terms, precision=HIGH).reshape(cols, scen)
        g_whole = lax.psum(g_local, "band")
        primal_next = jnp.clip(primal - eta * (cost_t - g_whole), 0.0, upper)
        extrapolated = 2.0 * primal_next - primal
        primal_slots = extrapolated.reshape(col_tiles, tile, scen)[col_index]
        fore_terms = jnp.einsum("sij,sjk->sik", scaled, primal_slots, precision=HIGH)
        h_local = jnp.einsum("rs,sik->rik", row_hot, fore_terms, precision=HIGH).reshape(rows, scen)
        share = rows // lax.axis_size("roster")
        begin = lax.axis_index("roster") * share
        h_share = lax.psum_scatter(h_local, "roster", scatter_dimension=0, tiled=True)
        own_dual = lax.dynamic_slice_in_dim(dual, begin, share, 0)
        own_rows = lax.dynamic_slice_in_dim(row_full, begin, share, 0)
        dual_share = own_dual + eta * (own_rows - h_share)
        dual = lax.all_gather(dual_share, "roster", axis=0, tiled=True)
        primal = primal_next
    return (primal, dual)


def solution(mesh):
    placed = (
        P("band", "roster", None, None, None),
        P("band", "roster", None),
        P("band", "roster"),
        P("roster", None),
        P("roster", None),
        P("band", None),
    )
    return jax.shard_map(
        shards,
        mesh=mesh,
        in_specs=placed,
        out_specs=(P("roster", None), P("band", None)),
        check_vma=False,
    )
```

profile of v0, /device:TPU:0, one launch (start us, length us, event | category | flops | bytes accessed | tf_op | source)
XLA Modules:
  0.0 466.0 jit_solution(17935510203944272796)
XLA Ops:
  7.9 0.7 fusion.89
  8.6 0.7 fusion.92
  10.5 1.8 fusion.3
  12.4 15.1 %pmax.43 = f32[512]{0:T(512)S(1)} all-reduce(f32[512]{0:T(512)S(1)} %bitcast.135), channel_id=1, replica_groups=mesh['band'=4,'roster'=8] {'roster'}, use_global_device_ids=true, to_apply=%region_5.6 | all-reduce | flops 512 | bytes 4096 | tf_op jit(solution)/shard_map/pmax | solution.py:49
  27.7 12.0 %pmax.42 = f32[768]{0:T(1024)S(1)} all-reduce(f32[768]{0:T(1024)S(1)} %reshape.279), channel_id=1, replica_groups=mesh['band'=4,'roster'=8] {'band'}, use_global_device_ids=true, to_apply=%region_2.3 | all-reduce | flops 768 | bytes 6144 | tf_op jit(solution)/shard_map/pmax | solution.py:50
  40.8 0.6 fusion.9
  41.6 8.4 %pmax.44 = f32[768]{0:T(1024)S(1)} all-reduce(f32[768]{0:T(1024)S(1)} %reshape.283), channel_id=1, replica_groups=mesh['band'=4,'roster'=8] {'band'}, use_global_device_ids=true, to_apply=%region_8.9 | all-reduce | flops 768 | bytes 6144 | tf_op jit(solution)/shard_map/pmax | solution.py:50
  50.0 11.8 %pmax.45 = f32[512]{0:T(512)S(1)} all-reduce(f32[512]{0:T(512)S(1)} %bitcast.136), channel_id=1, replica_groups=mesh['band'=4,'roster'=8] {'roster'}, use_global_device_ids=true, to_apply=%region_11.12 | all-reduce | flops 512 | bytes 4096 | tf_op jit(solution)/shard_map/pmax | solution.py:49
  63.0 0.6 fusion.14
  63.8 10.4 %pmax.46 = f32[768]{0:T(1024)S(1)} all-reduce(f32[768]{0:T(1024)S(1)} %reshape.287), channel_id=1, replica_groups=mesh['band'=4,'roster'=8] {'band'}, use_global_device_ids=true, to_apply=%region_14.15 | all-reduce | flops 768 | bytes 6144 | tf_op jit(solution)/shard_map/pmax | solution.py:50
  74.2 11.8 %pmax.47 = f32[512]{0:T(512)S(1)} all-reduce(f32[512]{0:T(512)S(1)} %bitcast.137), channel_id=1, replica_groups=mesh['band'=4,'roster'=8] {'roster'}, use_global_device_ids=true, to_apply=%region_17.18 | all-reduce | flops 512 | bytes 4096 | tf_op jit(solution)/shard_map/pmax | solution.py:49
  87.3 0.6 gather_fusion.8
  87.9 2.9 fusion.31
  90.9 1.0 fusion.49
  91.9 0.8 copy.19
  92.8 1.2 fusion.34
  93.9 37.9 %psum.35 = f32[]{:T(128)} all-reduce(f32[]{:T(128)} %fusion.34), channel_id=1, replica_groups=mesh['band'=4,'roster'=8] {'band','roster'}, use_global_device_ids=true, to_apply=%region_19.20 | all-reduce | flops 1 | bytes 8 | tf_op jit(solution)/shard_map/psum | solution.py:54
  132.6 1.3 multiply_subtract_fusion.3
  133.9 0.6 gather_fusion.9
  134.5 1.8 fusion.29
  136.3 1.0 fusion.47
  137.3 0.7 copy.21
  138.2 33.9 %reduce-scatter.5.cloned.1.call-done = f32[64,128]{1,0:T(8,128)} async-done(((f32[512,128]{1,0:T(8,128)}), f32[64,128]{1,0:T(8,128)}) %reduce-scatter.5.cloned.1.call-update) | async-done | bytes 32784 | tf_op jit(solution)/shard_map/reduce_scatter | solution.py:75
  172.0 0.8 multiply_add_fusion.3
  172.8 9.7 %all_gather.12 = f32[512,128]{1,0:T(8,128)S(1)} all-gather(f32[64,128]{1,0:T(8,128)S(1)} %multiply_add_fusion.3), channel_id=1, replica_groups=mesh['band'=4,'roster'=8] {'roster'}, dimensions={0}, use_global_device_ids=true | all-gather | bytes 294912 | tf_op jit(solution)/shard_map/all_gather | solution.py:79
  182.6 0.6 gather_fusion.10
  183.2 3.0 fusion.27
  186.1 1.0 fusion.45
  187.1 0.8 copy.24
  188.0 37.0 %all-reduce.7.cloned.1.call-done = f32[768,128]{1,0:T(8,128)} async-done(((f32[768,128]{1,0:T(8,128)}), f32[768,128]{1,0:T(8,128)}) %all-reduce.7.cloned.1.call-update) | async-done | bytes 393232 | tf_op jit(solution)/shard_map/psum | solution.py:67
  225.0 1.3 multiply_subtract_fusion.2
  226.3 0.6 gather_fusion.11
  226.9 1.8 fusion.25
  228.6 1.0 fusion.43
  229.6 0.7 copy.26
  230.4 33.5 %reduce-scatter.7.cloned.1.call-done = f32[64,128]{1,0:T(8,128)} async-done(((f32[512,128]{1,0:T(8,128)}), f32[64,128]{1,0:T(8,128)}) %reduce-scatter.7.cloned.1.call-update) | async-done | bytes 32784 | tf_op jit(solution)/shard_map/reduce_scatter | solution.py:75
  264.0 0.8 multiply_add_fusion.2
  264.8 9.4 %all_gather.13 = f32[512,128]{1,0:T(8,128)S(1)} all-gather(f32[64,128]{1,0:T(8,128)S(1)} %multiply_add_fusion.2), channel_id=1, replica_groups=mesh['band'=4,'roster'=8] {'roster'}, dimensions={0}, use_global_device_ids=true | all-gather | bytes 294912 | tf_op jit(solution)/shard_map/all_gather | solution.py:79
  274.2 0.6 gather_fusion.12
  274.8 3.0 fusion.23
  277.8 1.0 fusion.41
  278.8 0.8 copy.29
  279.6 37.1 %all-reduce.9.cloned.1.call-done = f32[768,128]{1,0:T(8,128)} async-done(((f32[768,128]{1,0:T(8,128)}), f32[768,128]{1,0:T(8,128)}) %all-reduce.9.cloned.1.call-update) | async-done | bytes 393232 | tf_op jit(solution)/shard_map/psum | solution.py:67
  316.7 1.3 multiply_subtract_fusion.1
  318.0 0.6 gather_fusion.13
  318.6 1.8 fusion.21
  320.3 1.0 fusion.39
  321.3 0.7 copy.31
  322.1 33.5 %reduce-scatter.9.cloned.1.call-done = f32[64,128]{1,0:T(8,128)} async-done(((f32[512,128]{1,0:T(8,128)}), f32[64,128]{1,0:T(8,128)}) %reduce-scatter.9.cloned.1.call-update) | async-done | bytes 32784 | tf_op jit(solution)/shard_map/reduce_scatter | solution.py:75
  355.7 0.8 multiply_add_fusion.1
  356.5 9.5 %all_gather.14 = f32[512,128]{1,0:T(8,128)S(1)} all-gather(f32[64,128]{1,0:T(8,128)S(1)} %multiply_add_fusion.1), channel_id=1, replica_groups=mesh['band'=4,'roster'=8] {'roster'}, dimensions={0}, use_global_device_ids=true | all-gather | bytes 294912 | tf_op jit(solution)/shard_map/all_gather | solution.py:79
  366.0 0.6 gather_fusion.14
  366.6 3.0 fusion.19
  369.5 1.0 fusion.37
  370.5 0.8 copy.34
  371.4 37.1 %all-reduce.11.cloned.1.call-done = f32[768,128]{1,0:T(8,128)} async-done(((f32[768,128]{1,0:T(8,128)}), f32[768,128]{1,0:T(8,128)}) %all-reduce.11.cloned.1.call-update) | async-done | bytes 393232 | tf_op jit(solution)/shard_map/psum | solution.py:67
  408.4 2.0 multiply_subtract_fusion
  411.1 1.8 fusion.17
  412.8 1.0 fusion.35
  413.8 0.7 copy.36
  414.6 33.6 %reduce-scatter.11.cloned.1.call-done = f32[64,128]{1,0:T(8,128)} async-done(((f32[512,128]{1,0:T(8,128)}), f32[64,128]{1,0:T(8,128)}) %reduce-scatter.11.cloned.1.call-update) | async-done | bytes 32784 | tf_op jit(solution)/shard_map/reduce_scatter | solution.py:75
  448.2 0.8 multiply_add_fusion
  449.0 9.2 %all_gather.15 = f32[512,128]{1,0:T(8,128)S(1)} all-gather(f32[64,128]{1,0:T(8,128)S(1)} %multiply_add_fusion), channel_id=1, replica_groups=mesh['band'=4,'roster'=8] {'roster'}, dimensions={0}, use_global_device_ids=true | all-gather | bytes 294912 | tf_op jit(solution)/shard_map/all_gather | solution.py:79
  458.2 0.7 copy.66
  (67 shorter events, 6.6 us)
Async XLA Ops:
  7.2 33.6 %copy-start = (bf16[1,1,6,256,256]{4,3,2,1,0:T(8,128)(2,1)S(1)}, bf16[1,1,6,256,256]{4,3,2,1,0:T(8,128)(2,1)}, u32[]{:S(2)}) copy-start(bf16[1,1,6,256,256]{4,3,2,1,0:T(8,128)(2,1)} %param.6) | copy-start | bytes 2359300
  7.2 125.4 %all-reduce.5.cloned.1.call-start = ((), (), s32[]{:S(2)}) async-start(), calls=%async_computation.4 | async-start | bytes 786432 | tf_op jit(solution)/shard_map/psum | solution.py:67
  41.4 45.7 %copy-start.3 = (f32[512,128]{1,0:T(8,128)S(1)}, f32[512,128]{1,0:T(8,128)}, u32[]{:S(2)}) copy-start(f32[512,128]{1,0:T(8,128)} %param.11) | copy-start | bytes 786436
  92.7 39.9 %copy-start.1 = (f32[768,128]{1,0:T(8,128)S(1)}, f32[768,128]{1,0:T(8,128)}, u32[]{:S(2)}) copy-start(f32[768,128]{1,0:T(8,128)} %param.9) | copy-start | bytes 1179652
  92.7 39.9 %copy-start.2 = (f32[768,128]{1,0:T(8,128)S(1)}, f32[768,128]{1,0:T(8,128)}, u32[]{:S(2)}) copy-start(f32[768,128]{1,0:T(8,128)} %param.10) | copy-start | bytes 1179652
  92.7 79.3 %reduce-scatter.5.cloned.1.call-start = ((), (), s32[]{:S(2)}) async-start(), calls=%async_computation.5 | async-start | bytes 294912 | tf_op jit(solution)/shard_map/reduce_scatter | solution.py:75
  138.0 87.0 %all-reduce.7.cloned.1.call-start = ((), (), s32[]{:S(2)}) async-start(), calls=%async_computation.6 | async-start | bytes 786432 | tf_op jit(solution)/shard_map/psum | solution.py:67
  187.9 76.1 %reduce-scatter.7.cloned.1.call-start = ((), (), s32[]{:S(2)}) async-start(), calls=%async_computation.7 | async-start | bytes 294912 | tf_op jit(solution)/shard_map/reduce_scatter | solution.py:75
  230.4 86.3 %all-reduce.9.cloned.1.call-start = ((), (), s32[]{:S(2)}) async-start(), calls=%async_computation.8 | async-start | bytes 786432 | tf_op jit(solution)/shard_map/psum | solution.py:67
  279.6 76.1 %reduce-scatter.9.cloned.1.call-start = ((), (), s32[]{:S(2)}) async-start(), calls=%async_computation.9 | async-start | bytes 294912 | tf_op jit(solution)/shard_map/reduce_scatter | solution.py:75
  322.1 86.4 %all-reduce.11.cloned.1.call-start = ((), (), s32[]{:S(2)}) async-start(), calls=%async_computation.10 | async-start | bytes 786432 | tf_op jit(solution)/shard_map/psum | solution.py:67
  371.3 76.8 %reduce-scatter.11.cloned.1.call-start = ((), (), s32[]{:S(2)}) async-start(), calls=%async_computation.11 | async-start | bytes 294912 | tf_op jit(solution)/shard_map/reduce_scatter | solution.py:75
Sparse Core Ops, SparseCore 0:
  92.8 33.2 all-reduce.4
  138.1 33.8 reduce-scatter.4
  188.0 36.9 all-reduce.6
  230.5 33.4 reduce-scatter.6
  279.7 36.9 all-reduce.8
  322.2 33.4 reduce-scatter.8
  371.5 36.9 all-reduce.10
  414.7 33.4 reduce-scatter.10
where the time goes:
time: 475 us; the launch traced here: 466 us
  waiting for transfers between devices  246 us (52%)
  blocking collectives  145 us (31%)
  matrix products  26.8 us (6%)
  local copies, waits for them, and re-layouts  16.3 us (3%)
  between operations  16.1 us (3%)
  other arithmetic  15.4 us (3%)
    reduce_scatter x4, waiting for transfers between devices, shards(): lax.psum_scatter(h_local, 'roster', scatter_dimension=0, tiled=True)  135 us
    psum x4, waiting for transfers between devices, shards(): g_whole = lax.psum(g_local, 'band')  111 us
    pmax x3, blocking collectives, shards(): row_peak = lax.pmax(row_peak, 'roster')  38.7 us
    psum x1, blocking collectives, shards(): squares = lax.psum(jnp.sum(scaled * scaled), ('band', 'roster'))  37.9 us
    all_gather x4, blocking collectives, shards(): dual = lax.all_gather(dual_share, 'roster', axis=0, tiled=True)  37.8 us
    pmax x3, blocking collectives, shards(): col_peak = lax.pmax(col_peak, 'band')  30.7 us
    dot_general x4, matrix products, shards(): back_terms = jnp.einsum('sij,sik->sjk', scaled, dual_slots, precision=HIGH)  11.8 us
  transfers between devices with their start and end apart: 8, of which 7 were waited for; matrix products, arithmetic and copies ran while one was open for 0% of the time, Pallas kernels for 0%

commit v1 on v0

--- a/solution.py
+++ b/solution.py
@@ -7,6 +7,28 @@
 ITERS = 4
 HIGH = lax.Precision.HIGHEST
 eps = 1e-06
+
+
+def joined_along(tiles, dim):
+    tiles = jnp.moveaxis(tiles, 0, dim)
+    shape = tiles.shape
+    return tiles.reshape(*shape[:dim], shape[dim] * shape[dim + 1], *shape[dim + 2 :])
+
+
+def gather_around(x, axis, dim):
+    size = lax.axis_size(axis)
+    pairs = [(i, (i + 1) % size) for i in range(size)]
+    back = [(b, a) for a, b in pairs]
+    lower, upper = ([], [])
+    for step in range(size - 1):
+        if step % 2 == 0:
+            lower.append(lax.ppermute(lower[-1] if lower else x, axis, pairs))
+        else:
+            upper.append(lax.ppermute(upper[-1] if upper else x, axis, back))
+    blocks = jnp.stack([*lower[::-1], x, *upper])
+    shift = lax.axis_index(axis) - len(lower)
+    blocks = blocks[(jnp.arange(size) - shift) % size]
+    return joined_along(blocks, dim)
 
 
 def shards(tiles, tile_slots, tile_count, costs, primal_start, dual_start):
@@ -76,7 +98,7 @@
         own_dual = lax.dynamic_slice_in_dim(dual, begin, share, 0)
         own_rows = lax.dynamic_slice_in_dim(row_full, begin, share, 0)
         dual_share = own_dual + eta * (own_rows - h_share)
-        dual = lax.all_gather(dual_share, "roster", axis=0, tiled=True)
+        dual = gather_around(dual_share, "roster", 0)
         primal = primal_next
     return (primal, dual)
 

time: 475 us -> 514 us (1.082)
  waiting for transfers between devices: 246 us -> 287 us
  blocking collectives: 145 us -> 107 us
  starting transfers between devices: 0.33 us -> 33 us
    all_gather x4 -> x0, blocking collectives: 37.8 us -> none  [shards(): dual = lax.all_gather(dual_share, 'roster', axis=0, tiled=True)]
    ppermute x0 -> x28, waiting for transfers between devices: none -> 37.1 us  [the longest x16 36.8 us: gather_around(): lower.append(lax.ppermute(lower[-1] if lower else x, axis, pairs))]
    ppermute x0 -> x28, starting transfers between devices: none -> 32.6 us  [the longest x12 32.1 us: gather_around(): upper.append(lax.ppermute(upper[-1] if upper else x, axis, back))]
  transfers between devices with their start and end apart: 8 -> 36, of which waited for: 7 -> 26; matrix products, arithmetic and copies ran while one was open for 0% -> 0% of each run, Pallas kernels for 0% -> 0%
where the time goes in v1:
time: 514 us; the launch traced here: 504 us
  waiting for transfers between devices  287 us (56%)
  blocking collectives  107 us (21%)
  starting transfers between devices  33 us (6%)
  matrix products  26.8 us (5%)
  local copies, waits for them, and re-layouts  18.7 us (4%)
  between operations  16.4 us (3%)
  other arithmetic  15.5 us (3%)
    reduce_scatter x4, waiting for transfers between devices, shards(): lax.psum_scatter(h_local, 'roster', scatter_dimension=0, tiled=True)  134 us
    psum x4, waiting for transfers between devices, shards(): g_whole = lax.psum(g_local, 'band')  115 us
    pmax x3, blocking collectives, shards(): row_peak = lax.pmax(row_peak, 'roster')  38.7 us
    psum x1, blocking collectives, shards(): squares = lax.psum(jnp.sum(scaled * scaled), ('band', 'roster'))  38 us
    ppermute x16, waiting for transfers between devices, gather_around(): lower.append(lax.ppermute(lower[-1] if lower else x, axis, pairs))  36.8 us
    ppermute x12, starting transfers between devices, gather_around(): upper.append(lax.ppermute(upper[-1] if upper else x, axis, back))  32.1 us
    pmax x3, blocking collectives, shards(): col_peak = lax.pmax(col_peak, 'band')  30.7 us
    dot_general x4, matrix products, shards(): back_terms = jnp.einsum('sij,sik->sjk', scaled, dual_slots, precision=HIGH)  11.8 us
  transfers between devices with their start and end apart: 36, of which 26 were waited for; matrix products, arithmetic and copies ran while one was open for 0% of the time, Pallas kernels for 0%

profile of v1, /device:TPU:0, one launch (start us, length us, event | category | flops | bytes accessed | tf_op | source)
XLA Modules:
  0.0 504.3 jit_solution(9852510937252173067)
XLA Ops:
  10.5 1.8 fusion.3
  12.4 15.1 %pmax.43 = f32[512]{0:T(512)S(1)} all-reduce(f32[512]{0:T(512)S(1)} %bitcast.209), channel_id=1, replica_groups=mesh['band'=4,'roster'=8] {'roster'}, use_global_device_ids=true, to_apply=%region_5.6 | all-reduce | flops 512 | bytes 4096 | tf_op jit(solution)/shard_map/pmax | solution.py:71
  27.7 12.0 %pmax.42 = f32[768]{0:T(1024)S(1)} all-reduce(f32[768]{0:T(1024)S(1)} %reshape.331), channel_id=1, replica_groups=mesh['band'=4,'roster'=8] {'band'}, use_global_device_ids=true, to_apply=%region_2.3 | all-reduce | flops 768 | bytes 6144 | tf_op jit(solution)/shard_map/pmax | solution.py:72
  41.6 8.4 %pmax.44 = f32[768]{0:T(1024)S(1)} all-reduce(f32[768]{0:T(1024)S(1)} %reshape.335), channel_id=1, replica_groups=mesh['band'=4,'roster'=8] {'band'}, use_global_device_ids=true, to_apply=%region_8.9 | all-reduce | flops 768 | bytes 6144 | tf_op jit(solution)/shard_map/pmax | solution.py:72
  50.0 11.8 %pmax.45 = f32[512]{0:T(512)S(1)} all-reduce(f32[512]{0:T(512)S(1)} %bitcast.210), channel_id=1, replica_groups=mesh['band'=4,'roster'=8] {'roster'}, use_global_device_ids=true, to_apply=%region_11.12 | all-reduce | flops 512 | bytes 4096 | tf_op jit(solution)/shard_map/pmax | solution.py:71
  63.8 10.4 %pmax.46 = f32[768]{0:T(1024)S(1)} all-reduce(f32[768]{0:T(1024)S(1)} %reshape.339), channel_id=1, replica_groups=mesh['band'=4,'roster'=8] {'band'}, use_global_device_ids=true, to_apply=%region_14.15 | all-reduce | flops 768 | bytes 6144 | tf_op jit(solution)/shard_map/pmax | solution.py:72
  74.2 11.8 %pmax.47 = f32[512]{0:T(512)S(1)} all-reduce(f32[512]{0:T(512)S(1)} %bitcast.211), channel_id=1, replica_groups=mesh['band'=4,'roster'=8] {'roster'}, use_global_device_ids=true, to_apply=%region_17.18 | all-reduce | flops 512 | bytes 4096 | tf_op jit(solution)/shard_map/pmax | solution.py:71
  87.9 2.9 fusion.31
  90.9 1.0 fusion.49
  92.8 1.2 fusion.34
  93.9 38.0 %psum.35 = f32[]{:T(128)} all-reduce(f32[]{:T(128)} %fusion.34), channel_id=1, replica_groups=mesh['band'=4,'roster'=8] {'band','roster'}, use_global_device_ids=true, to_apply=%region_19.20 | all-reduce | flops 1 | bytes 8 | tf_op jit(solution)/shard_map/psum | solution.py:76
  132.6 1.3 multiply_subtract_fusion.3
  134.5 1.8 fusion.29
  138.2 33.8 %reduce-scatter.5.cloned.1.call-done = f32[64,128]{1,0:T(8,128)} async-done(((f32[512,128]{1,0:T(8,128)}), f32[64,128]{1,0:T(8,128)}) %reduce-scatter.5.cloned.1.call-update) | async-done | bytes 32784 | tf_op jit(solution)/shard_map/reduce_scatter | solution.py:97
  173.3 4.2 collective-permute-done
  177.5 2.6 collective-permute-start.4
  180.2 1.9 collective-permute-done.1
  182.1 2.7 collective-permute-start.5
  184.8 1.5 collective-permute-done.2
  186.4 2.6 collective-permute-start.6
  189.0 1.5 collective-permute-done.3
  191.8 2.9 fusion.27
  194.8 1.0 fusion.45
  196.7 38.3 %all-reduce.7.cloned.1.call-done = f32[768,128]{1,0:T(8,128)} async-done(((f32[768,128]{1,0:T(8,128)}), f32[768,128]{1,0:T(8,128)}) %all-reduce.7.cloned.1.call-update) | async-done | bytes 393232 | tf_op jit(solution)/shard_map/psum | solution.py:89
  234.9 1.3 multiply_subtract_fusion.2
  236.8 1.8 fusion.25
  238.6 1.0 fusion.43
  240.4 33.5 %reduce-scatter.7.cloned.1.call-done = f32[64,128]{1,0:T(8,128)} async-done(((f32[512,128]{1,0:T(8,128)}), f32[64,128]{1,0:T(8,128)}) %reduce-scatter.7.cloned.1.call-update) | async-done | bytes 32784 | tf_op jit(solution)/shard_map/reduce_scatter | solution.py:97
  274.8 4.2 collective-permute-done.7
  279.0 2.6 collective-permute-start.11
  281.6 1.9 collective-permute-done.8
  283.6 2.6 collective-permute-start.12
  286.2 1.6 collective-permute-done.9
  287.8 2.8 collective-permute-start.13
  290.6 1.4 collective-permute-done.10
  293.4 3.0 fusion.23
  296.3 1.0 fusion.41
  298.2 38.3 %all-reduce.9.cloned.1.call-done = f32[768,128]{1,0:T(8,128)} async-done(((f32[768,128]{1,0:T(8,128)}), f32[768,128]{1,0:T(8,128)}) %all-reduce.9.cloned.1.call-update) | async-done | bytes 393232 | tf_op jit(solution)/shard_map/psum | solution.py:89
  336.5 1.3 multiply_subtract_fusion.1
  338.3 1.8 fusion.21
  340.1 1.0 fusion.39
  341.9 33.5 %reduce-scatter.9.cloned.1.call-done = f32[64,128]{1,0:T(8,128)} async-done(((f32[512,128]{1,0:T(8,128)}), f32[64,128]{1,0:T(8,128)}) %reduce-scatter.9.cloned.1.call-update) | async-done | bytes 32784 | tf_op jit(solution)/shard_map/reduce_scatter | solution.py:97
  376.3 4.2 collective-permute-done.14
  380.5 2.6 collective-permute-start.18
  383.2 1.9 collective-permute-done.15
  385.1 2.6 collective-permute-start.19
  387.7 1.6 collective-permute-done.16
  389.3 2.8 collective-permute-start.20
  392.2 1.4 collective-permute-done.17
  394.9 3.0 fusion.19
  397.9 1.0 fusion.37
  399.7 38.3 %all-reduce.11.cloned.1.call-done = f32[768,128]{1,0:T(8,128)} async-done(((f32[768,128]{1,0:T(8,128)}), f32[768,128]{1,0:T(8,128)}) %all-reduce.11.cloned.1.call-update) | async-done | bytes 393232 | tf_op jit(solution)/shard_map/psum | solution.py:89
  438.0 2.0 multiply_subtract_fusion
  440.7 1.8 fusion.17
  442.4 1.0 fusion.35
  444.2 33.6 %reduce-scatter.11.cloned.1.call-done = f32[64,128]{1,0:T(8,128)} async-done(((f32[512,128]{1,0:T(8,128)}), f32[64,128]{1,0:T(8,128)}) %reduce-scatter.11.cloned.1.call-update) | async-done | bytes 32784 | tf_op jit(solution)/shard_map/reduce_scatter | solution.py:97
  478.6 4.2 collective-permute-done.21
  482.8 2.6 collective-permute-start.25
  485.5 1.9 collective-permute-done.22
  487.4 2.6 collective-permute-start.26
  490.0 1.6 collective-permute-done.23
  491.6 2.6 collective-permute-start.27
  494.3 1.6 collective-permute-done.24
  496.0 1.3 gather_fusion.19
  (156 shorter events, 26.4 us)
Async XLA Ops:
  7.2 33.6 %copy-start = (bf16[1,1,6,256,256]{4,3,2,1,0:T(8,128)(2,1)S(1)}, bf16[1,1,6,256,256]{4,3,2,1,0:T(8,128)(2,1)}, u32[]{:S(2)}) copy-start(bf16[1,1,6,256,256]{4,3,2,1,0:T(8,128)(2,1)} %param.6) | copy-start | bytes 2359300
  7.2 125.4 %all-reduce.5.cloned.1.call-start = ((), (), s32[]{:S(2)}) async-start(), calls=%async_computation.4 | async-start | bytes 786432 | tf_op jit(solution)/shard_map/psum | solution.py:89
  41.4 45.7 %copy-start.3 = (f32[512,128]{1,0:T(8,128)S(1)}, f32[512,128]{1,0:T(8,128)}, u32[]{:S(2)}) copy-start(f32[512,128]{1,0:T(8,128)} %param.11) | copy-start | bytes 786436
  92.7 39.9 %copy-start.1 = (f32[768,128]{1,0:T(8,128)S(1)}, f32[768,128]{1,0:T(8,128)}, u32[]{:S(2)}) copy-start(f32[768,128]{1,0:T(8,128)} %param.9) | copy-start | bytes 1179652
  92.7 40.0 %copy-start.2 = (f32[768,128]{1,0:T(8,128)S(1)}, f32[768,128]{1,0:T(8,128)}, u32[]{:S(2)}) copy-start(f32[768,128]{1,0:T(8,128)} %param.10) | copy-start | bytes 1179652
  92.7 79.3 %reduce-scatter.5.cloned.1.call-start = ((), (), s32[]{:S(2)}) async-start(), calls=%async_computation.5 | async-start | bytes 294912 | tf_op jit(solution)/shard_map/reduce_scatter | solution.py:97
  138.0 96.9 %all-reduce.7.cloned.1.call-start = ((), (), s32[]{:S(2)}) async-start(), calls=%async_computation.6 | async-start | bytes 786432 | tf_op jit(solution)/shard_map/psum | solution.py:89
  172.8 4.7 collective-permute-start
  177.5 4.5 collective-permute-start.1
  177.5 4.6 collective-permute-start.4
  182.1 4.2 collective-permute-start.2
  182.1 4.3 collective-permute-start.5
  186.3 4.2 collective-permute-start.3
  186.4 4.2 collective-permute-start.6
  196.6 77.3 %reduce-scatter.7.cloned.1.call-start = ((), (), s32[]{:S(2)}) async-start(), calls=%async_computation.7 | async-start | bytes 294912 | tf_op jit(solution)/shard_map/reduce_scatter | solution.py:97
  240.3 96.1 %all-reduce.9.cloned.1.call-start = ((), (), s32[]{:S(2)}) async-start(), calls=%async_computation.8 | async-start | bytes 786432 | tf_op jit(solution)/shard_map/psum | solution.py:89
  274.7 4.2 collective-permute-start.7
  279.0 4.6 collective-permute-start.8
  279.0 4.6 collective-permute-start.11
  283.5 4.2 collective-permute-start.9
  283.6 4.2 collective-permute-start.12
  287.8 4.2 collective-permute-start.10
  287.8 4.4 collective-permute-start.13
  298.1 77.3 %reduce-scatter.9.cloned.1.call-start = ((), (), s32[]{:S(2)}) async-start(), calls=%async_computation.9 | async-start | bytes 294912 | tf_op jit(solution)/shard_map/reduce_scatter | solution.py:97
  341.9 96.2 %all-reduce.11.cloned.1.call-start = ((), (), s32[]{:S(2)}) async-start(), calls=%async_computation.10 | async-start | bytes 786432 | tf_op jit(solution)/shard_map/psum | solution.py:89
  376.3 4.2 collective-permute-start.14
  380.5 4.5 collective-permute-start.15
  380.5 4.6 collective-permute-start.18
  385.1 4.2 collective-permute-start.16
  385.1 4.2 collective-permute-start.19
  389.3 4.2 collective-permute-start.17
  389.3 4.4 collective-permute-start.20
  399.7 78.1 %reduce-scatter.11.cloned.1.call-start = ((), (), s32[]{:S(2)}) async-start(), calls=%async_computation.11 | async-start | bytes 294912 | tf_op jit(solution)/shard_map/reduce_scatter | solution.py:97
  478.6 4.2 collective-permute-start.21
  482.8 4.5 collective-permute-start.22
  482.8 4.5 collective-permute-start.25
  487.4 4.2 collective-permute-start.23
  487.4 4.2 collective-permute-start.26
  491.6 4.2 collective-permute-start.24
  491.6 4.3 collective-permute-start.27
Sparse Core Ops, SparseCore 0:
  92.8 33.2 all-reduce.4
  138.2 33.7 reduce-scatter.4
  196.7 38.1 all-reduce.6
  240.4 33.4 reduce-scatter.6
  298.2 38.1 all-reduce.8
  342.0 33.4 reduce-scatter.8
  399.8 38.1 all-reduce.10
  444.3 33.4 reduce-scatter.10
